TPU v7x, 32 devices: a whole 2x2x4 slice. The times are simulated.
32 devices in a mesh: row: 8 (over z, y), col: 4 (over x, core).
Axes of the slice: x: 2, y: 2, z: 4, core: 2. Of those that a mesh axis runs over, the one named last changes fastest.
Arguments:
- trailing: bfloat16 [12288, 12288], P('row', 'col'), may hold values from -6 to 6
- rows_a: int32 [8, 12], replicated, may hold values from 0 to 11, as said below
- counts_a: int32 [8], replicated, may hold values from 1 to 12, as said below
- factor_a: bfloat16 [12288, 512], P('row'), may hold values from -0.0546875 to 0.0546875
- rows_b: int32 [8, 12], replicated, may hold values from 0 to 11, as said below
- counts_b: int32 [8], replicated, may hold values from 1 to 12, as said below
- factor_b: bfloat16 [12288, 512], P('row'), may hold values from -0.0546875 to 0.0546875
- factor_top: bfloat16 [512, 512], replicated, may hold values from -0.25 to 0.25
- base_a: float32 [512, 512], P('col'), may hold values from -3 to 3
- base_b: float32 [512, 512], P('col'), may hold values from -3 to 3
Outputs:
- column_a: bfloat16 [12288, 512], P('row')
- diag_a: float32 [512, 512], P('col')
- column_b: bfloat16 [12288, 512], P('row')
- top_b: bfloat16 [512, 512], P('col')
- diag_b: float32 [512, 512], P('col')
Inputs may be any that keep to these rules, and one draw needn't show every extreme that they name: `rows_a`: the first counts_a[r] entries of row r are distinct; the rest of the row is padding. `counts_a`: some owner uses all 12 slots in every draw. `rows_b`: the first counts_b[r] entries of row r are distinct and lie among the first counts_a[r] entries of row r of rows_a; the rest is padding. counts_b[r] <= counts_a[r]; some owner uses all 12 slots in every draw.
All inputs are finite; a program needn't handle non-finite values.
Results may differ from a plain program's by a relative error of at most 0.007.
Values may be sent and summed in bfloat16 or wider, within the bound.
A program may use at most 128 MiB of HBM per device.

v0:
```python
import jax
import jax.numpy as jnp
from jax import lax
from jax.sharding import PartitionSpec as P

BS = 128
W = 512
RBD = 12
PAD = 12


def spread_2(value, axis, source):
    kept = jnp.where(lax.axis_index(axis) == source, value, 0).astype(value.dtype)
    return lax.psum(kept, axis)


def contract_rows(former, latter):
    return lax.dot_general(
        former, latter, (((0,), (0,)), ((), ())), preferred_element_type=jnp.float32
    )


def slot_live(counts, owner_idx):
    live_count = lax.dynamic_index_in_dim(counts, owner_idx, 0, keepdims=False)
    return jnp.arange(PAD, dtype=jnp.int32) < live_count


def on_device(
    trailing, rows_a, counts_a, factor_a, rows_b, counts_b, factor_b, factor_top, base_a, base_b
):
    row_count = lax.axis_size("row")
    col_count = lax.axis_size("col")
    fanout = row_count // col_count
    row_index = lax.axis_index("row")
    col_index = lax.axis_index("col")
    col_blocks = trailing.shape[1] // BS
    part_width = W // col_count
    slot_rows = PAD * BS
    share_rows = slot_rows // col_count
    width_start = col_index * part_width
    share_start = col_index * share_rows
    slab_blocks = trailing.reshape(RBD, BS, trailing.shape[1])

    def row_gate(live_rows):
        return jnp.repeat(live_rows.astype(jnp.float32), BS)[:, None]

    def partial_product(rows, counts, factor):
        own_rows = lax.dynamic_index_in_dim(rows, row_index, 0, keepdims=False)
        row_slab = jnp.take(slab_blocks, own_rows, axis=0).reshape(slot_rows, trailing.shape[1])
        pieces = []
        targets = []
        flags = []
        for offset in range(fanout):
            source = col_index + offset * col_count
            pieces.append(spread_2(factor, "row", source))
            src_rows = lax.dynamic_index_in_dim(rows, source, 0, keepdims=False)
            targets.append(src_rows * fanout + offset)
            flags.append(slot_live(counts, source))
        received = jnp.stack(pieces).reshape(fanout * PAD, BS * W)
        target = jnp.concatenate(targets)
        live_src = jnp.concatenate(flags)
        selector = (
            (jnp.arange(col_blocks, dtype=jnp.int32)[:, None] == target[None, :])
            & live_src[None, :]
        ).astype(jnp.bfloat16)
        spread = jnp.dot(selector, received, preferred_element_type=jnp.float32).astype(
            jnp.bfloat16
        )
        return jnp.dot(
            row_slab, spread.reshape(col_blocks * BS, W), preferred_element_type=jnp.float32
        )

    def finish(partial_value, live_rows, addend):
        gate = row_gate(live_rows)
        reduced = lax.psum_scatter(partial_value, "col", scatter_dimension=0, tiled=True)
        if addend is not None:
            reduced = reduced + addend(share_start, share_rows)
        share_gate = lax.dynamic_slice_in_dim(gate, share_start, share_rows, 0)
        share_out = (-reduced * share_gate).astype(jnp.bfloat16)
        return lax.all_gather(share_out, "col", axis=0, tiled=True)

    def row_sums(pieces_in):
        return lax.psum(pieces_in, "row")

    live_a = slot_live(counts_a, row_index)
    live_b = slot_live(counts_b, row_index)
    column_a = finish(partial_product(rows_a, counts_a, factor_a), live_a, None)
    own_rows_a = lax.dynamic_index_in_dim(rows_a, row_index, 0, keepdims=False)
    own_rows_b = lax.dynamic_index_in_dim(rows_b, row_index, 0, keepdims=False)
    pairing = (
        (own_rows_b[:, None] == own_rows_a[None, :]) & live_a[None, :] & live_b[:, None]
    ).astype(jnp.bfloat16)
    carried = (
        jnp.dot(pairing, column_a.reshape(PAD, BS * W), preferred_element_type=jnp.float32)
        .astype(jnp.bfloat16)
        .reshape(slot_rows, W)
    )
    width_a = lax.dynamic_slice_in_dim(column_a, width_start, part_width, 1)
    width_c = lax.dynamic_slice_in_dim(carried, width_start, part_width, 1)
    sums_a = row_sums((contract_rows(width_a, factor_a), contract_rows(width_c, factor_b)))
    diag_a = base_a - sums_a[0]
    top_b = (
        -(
            sums_a[1]
            + jnp.dot(diag_a, factor_top.astype(jnp.float32), precision=lax.Precision.HIGHEST)
        )
    ).astype(jnp.bfloat16)

    def cross_rows(first_row, row_total):
        picked = lax.dynamic_slice_in_dim(carried, first_row, row_total, 0)
        return jnp.dot(picked, factor_top, preferred_element_type=jnp.float32)

    column_b = finish(partial_product(rows_b, counts_b, factor_b), live_b, cross_rows)
    width_b = lax.dynamic_slice_in_dim(column_b, width_start, part_width, 1)
    sums_b = row_sums((contract_rows(width_b, factor_b),))
    top_whole = lax.all_gather(top_b, "col", axis=0, tiled=True)
    top_cols = lax.dynamic_slice_in_dim(top_whole, width_start, part_width, 1)
    diag_b = base_b - sums_b[0] - contract_rows(top_cols, factor_top)
    return (column_a, diag_a, column_b, top_b, diag_b)


def solution(mesh):
    in_specs = (
        P("row", "col"),
        P(),
        P(),
        P("row", None),
        P(),
        P(),
        P("row", None),
        P(),
        P("col", None),
        P("col", None),
    )
    out_specs = (P("row", None), P("col", None), P("row", None), P("col", None), P("col", None))
    return jax.shard_map(
        on_device, mesh=mesh, in_specs=in_specs, out_specs=out_specs, check_vma=False
    )
```

profile of v0, /device:TPU:0, one launch (start us, length us, event | category | flops | bytes accessed | tf_op | source)
XLA Modules:
  0.0 484.4 jit_solution(11630658327107411684)
XLA Ops:
  7.2 4.8 select_bitcast_fusion.1
  13.5 9.4 %gather_fusion = bf16[12,128,3072]{2,1,0:T(8,128)(2,1)} fusion(bf16[12,128,3072]{2,1,0:T(8,128)(2,1)} %bitcast.59, s32[1024]{0:T(1024)S(1)} %pad_clamp_fusion.1), kind=kCustom, calls=%fused_computation.clone | custom fusion | bytes 18874416 | tf_op jit(solution)/shard_map/jit(_take)/gather | solution.py:49
  26.7 8.4 %broadcast_select_fusion.1 = bf16[12,128,3072]{2,1,0:T(8,128)(2,1)} fusion(bf16[12,128,3072]{2,1,0:T(8,128)(2,1)} %gather_fusion, pred[12]{0:T(512)(128)(4,1)S(1)} %get-tuple-element.15), kind=kLoop, calls=%fused_computation.6 | loop fusion | flops 4718592 | bytes 18874380 | tf_op jit(solution)/shard_map/jit(_take)/select_n | solution.py:49
  35.0 191.1 %all-reduce.7.cloned.1.call-done = (bf16[1,1536,512]{2,1,0:T(8,128)(2,1)}, bf16[1,1536,512]{2,1,0:T(8,128)(2,1)}, bf16[1,1536,512]{2,1,0:T(8,128)(2,1)}, bf16[1,1536,512]{2,1,0:T(8,128)(2,1)}) async-done(((bf16[1,1536,512]{2,1,0:T(8,128)(2,1)}, bf16[1,1536,512]{2,1,0:T(8,128)(2,1)}, bf16[1,1536,512]{2,1,0:T(8,128)(2,1)}, bf16[1,1536,512]{2,1,0:T(8,128)(2,1)}), (bf16[1,1536,512]{2,1,0:T(8,128)(2,1)}, ...) | async-done | bytes 6291472 | tf_op jit(solution)/shard_map/psum | solution.py:14
  226.1 3.8 pad_maximum_fusion
  229.9 5.2 %reshape.70 = bf16[24,65536]{1,0:T(8,128)(2,1)} reshape(bf16[2,1536,512]{2,1,0:T(8,128)(2,1)} %pad_maximum_fusion) | data formatting | bytes 6291456 | tf_op jit(solution)/shard_map/reshape | solution.py:59
  235.1 4.5 convolution_convert_fusion.1
  239.6 5.2 %reshape.71 = bf16[3072,512]{1,0:T(8,128)(2,1)} reshape(bf16[24,65536]{1,0:T(8,128)(2,1)} %convolution_convert_fusion.1) | data formatting | bytes 6291456 | tf_op jit(solution)/shard_map/reshape | solution.py:70
  244.8 10.6 %fusion.53 = f32[1536,512]{1,0:T(8,128)} fusion(bf16[1536,3072]{1,0:T(8,128)(2,1)} %bitcast.62, bf16[3072,512]{1,0:T(8,128)(2,1)} %reshape.71), kind=kOutput, calls=%fused_computation.96 | convolution fusion | flops 4831838208 | bytes 15728640 | tf_op jit(solution)/shard_map/dot_general | solution.py:69
  255.5 9.7 %gather_fusion.1 = bf16[12,128,3072]{2,1,0:T(8,128)(2,1)} fusion(bf16[12,128,3072]{2,1,0:T(8,128)(2,1)} %bitcast.60, s32[1024]{0:T(1024)S(1)} %pad_clamp_fusion), kind=kCustom, calls=%fused_computation.1.clone | custom fusion | bytes 18874416 | tf_op jit(solution)/shard_map/jit(_take)/gather | solution.py:49
  267.3 8.4 %broadcast_select_fusion = bf16[12,128,3072]{2,1,0:T(8,128)(2,1)} fusion(bf16[12,128,3072]{2,1,0:T(8,128)(2,1)} %gather_fusion.1, pred[12]{0:T(512)(128)(4,1)S(1)} %get-tuple-element.13), kind=kLoop, calls=%fused_computation.5 | loop fusion | flops 4718592 | bytes 18874380 | tf_op jit(solution)/shard_map/jit(_take)/select_n | solution.py:49
  275.8 16.7 %reduce-scatter.3.cloned.1.call-done = f32[384,512]{1,0:T(8,128)} async-done(((f32[1536,512]{1,0:T(8,128)}), f32[384,512]{1,0:T(8,128)}) %reduce-scatter.3.cloned.1.call-update) | async-done | bytes 786448 | tf_op jit(solution)/shard_map/reduce_scatter | solution.py:75
  294.8 3.4 pad_maximum_fusion.1
  298.1 5.2 %reshape.73 = bf16[24,65536]{1,0:T(8,128)(2,1)} reshape(bf16[2,1536,512]{2,1,0:T(8,128)(2,1)} %pad_maximum_fusion.1) | data formatting | bytes 6291456 | tf_op jit(solution)/shard_map/reshape | solution.py:59
  303.3 4.5 convolution_convert_fusion
  307.9 5.2 %reshape.74 = bf16[3072,512]{1,0:T(8,128)(2,1)} reshape(bf16[24,65536]{1,0:T(8,128)(2,1)} %convolution_convert_fusion) | data formatting | bytes 6291456 | tf_op jit(solution)/shard_map/reshape | solution.py:70
  313.0 10.6 %fusion.54 = f32[1536,512]{1,0:T(8,128)} fusion(bf16[1536,3072]{1,0:T(8,128)(2,1)} %bitcast.61, bf16[3072,512]{1,0:T(8,128)(2,1)} %reshape.74), kind=kOutput, calls=%fused_computation.97 | convolution fusion | flops 4831838208 | bytes 15728640 | tf_op jit(solution)/shard_map/dot_general | solution.py:69
  330.1 3.6 reshape.76
  333.7 28.0 %reduce-scatter.5.cloned.1.call-done = f32[384,512]{1,0:T(8,128)} async-done(((f32[1536,512]{1,0:T(8,128)}), f32[384,512]{1,0:T(8,128)}) %reduce-scatter.5.cloned.1.call-update) | async-done | bytes 786448 | tf_op jit(solution)/shard_map/reduce_scatter | solution.py:75
  361.7 2.4 fusion.2
  366.3 2.7 fusion.10
  369.0 14.9 %all-gather.5.cloned.1.call-done = bf16[1536,512]{1,0:T(8,128)(2,1)} async-done(((bf16[384,512]{1,0:T(8,128)(2,1)}), bf16[1536,512]{1,0:T(8,128)(2,1)}) %all-gather.5.cloned.1.call-update) | async-done | bytes 1572880 | tf_op jit(solution)/shard_map/all_gather | solution.py:80
  386.1 77.7 %all-reduce.5.cloned.1.call-done = (f32[128,512]{1,0:T(8,128)}, f32[128,512]{1,0:T(8,128)}, f32[128,512]{1,0:T(8,128)}) async-done(((f32[128,512]{1,0:T(8,128)}, f32[128,512]{1,0:T(8,128)}, f32[128,512]{1,0:T(8,128)}), (f32[128,512]{1,0:T(8,128)}, f32[128,512]{1,0:T(8,128)}, f32[128,512]{1,0:T(8,128)})) %all-reduce.5.cloned.1.call-update) | async-done | bytes 786448 | tf_op jit(solution)/shard_map/psum | solution.py:83
  466.2 7.2 %all_gather.11 = bf16[512,512]{1,0:T(8,128)(2,1)S(1)} all-gather(bf16[128,512]{1,0:T(8,128)(2,1)S(1)} %fusion.4), channel_id=1, replica_groups=mesh['row'=8,'col'=4] {'col'}, dimensions={0}, use_global_device_ids=true | all-gather | bytes 655360 | tf_op jit(solution)/shard_map/all_gather | solution.py:116
  (70 shorter events, 27.0 us)
Async XLA Ops:
  7.2 354.6 %copy-start = (bf16[512,512]{1,0:T(8,128)(2,1)S(1)}, bf16[512,512]{1,0:T(8,128)(2,1)}, u32[]{:S(2)}) copy-start(bf16[512,512]{1,0:T(8,128)(2,1)} %param.19) | copy-start | bytes 1572868
  7.2 218.9 %all-reduce.7.cloned.1.call-start = ((), (), s32[]{:S(2)}) async-start(), calls=%async_computation.7 | async-start | bytes 12582912 | tf_op jit(solution)/shard_map/psum | solution.py:14
  12.0 280.5 %reduce-scatter.3.cloned.1.call-start = ((), (), s32[]{:S(2)}) async-start(), calls=%async_computation.2 | async-start | bytes 3932160 | tf_op jit(solution)/shard_map/reduce_scatter | solution.py:75
  13.5 9.5 %copy-start.9 = (s32[8]{0:T(128)S(1)}, s32[8]{0:T(128)}, u32[]{:S(2)}) copy-start(s32[8]{0:T(128)} %param.17) | copy-start | bytes 100
  13.5 9.4 %copy-start.10 = (s32[8]{0:T(128)S(1)}, s32[8]{0:T(128)}, u32[]{:S(2)}) copy-start(s32[8]{0:T(128)} %param.14) | copy-start | bytes 100
  255.4 70.4 %all-gather.3.cloned.1.call-start = ((), (), s32[]{:S(2)}) async-start(), calls=%async_computation.3 | async-start | bytes 1966080 | tf_op jit(solution)/shard_map/all_gather | solution.py:80
  267.3 27.5 %copy-start.4 = (bf16[1,1536,512]{2,1,0:T(8,128)(2,1)S(1)}, bf16[1,1536,512]{2,1,0:T(8,128)(2,1)}, u32[]{:S(2)}) copy-start(bf16[1,1536,512]{2,1,0:T(8,128)(2,1)} %get-tuple-element.11) | copy-start | bytes 4718596
  294.5 67.2 %reduce-scatter.5.cloned.1.call-start = ((), (), s32[]{:S(2)}) async-start(), calls=%async_computation.4 | async-start | bytes 3932160 | tf_op jit(solution)/shard_map/reduce_scatter | solution.py:75
  323.7 60.3 %all-gather.5.cloned.1.call-start = ((), (), s32[]{:S(2)}) async-start(), calls=%async_computation.5 | async-start | bytes 1966080 | tf_op jit(solution)/shard_map/all_gather | solution.py:80
  330.1 34.1 %copy-start.1 = (bf16[1536,512]{1,0:T(8,128)(2,1)S(1)}, bf16[1536,512]{1,0:T(8,128)(2,1)}, u32[]{:S(2)}) copy-start(bf16[1536,512]{1,0:T(8,128)(2,1)} %param.18) | copy-start | bytes 4718596
  364.1 99.6 %all-reduce.5.cloned.1.call-start = ((), (), s32[]{:S(2)}) async-start(), calls=%async_computation.6 | async-start | bytes 1572864 | tf_op jit(solution)/shard_map/psum | solution.py:83
  366.3 97.4 %copy-start.7 = (f32[128,512]{1,0:T(8,128)S(1)}, f32[128,512]{1,0:T(8,128)}, u32[]{:S(2)}) copy-start(f32[128,512]{1,0:T(8,128)} %param.20) | copy-start | bytes 786436
  369.0 104.4 %copy-start.8 = (f32[128,512]{1,0:T(8,128)S(1)}, f32[128,512]{1,0:T(8,128)}, u32[]{:S(2)}) copy-start(f32[128,512]{1,0:T(8,128)} %param.21) | copy-start | bytes 786436
  386.0 89.3 %copy-start.2 = (bf16[1536,512]{1,0:T(8,128)(2,1)S(1)}, bf16[1536,512]{1,0:T(8,128)(2,1)}, u32[]{:S(2)}) copy-start(bf16[1536,512]{1,0:T(8,128)(2,1)} %all-gather.3.cloned.1.call-done) | copy-start | bytes 4718596
  464.7 11.7 %copy-start.5 = (f32[128,512]{1,0:T(8,128)}, f32[128,512]{1,0:T(8,128)S(1)}, u32[]{:S(2)}) copy-start(f32[128,512]{1,0:T(8,128)S(1)} %sub.9) | copy-start | bytes 786436
  464.7 11.7 %copy-start.3 = (bf16[1536,512]{1,0:T(8,128)(2,1)S(1)}, bf16[1536,512]{1,0:T(8,128)(2,1)}, u32[]{:S(2)}) copy-start(bf16[1536,512]{1,0:T(8,128)(2,1)} %all-gather.5.cloned.1.call-done) | copy-start | bytes 4718596
  466.2 11.4 %copy-start.6 = (bf16[128,512]{1,0:T(8,128)(2,1)}, bf16[128,512]{1,0:T(8,128)(2,1)S(1)}, u32[]{:S(2)}) copy-start(bf16[128,512]{1,0:T(8,128)(2,1)S(1)} %fusion.4) | copy-start | bytes 393220
Sparse Core Ops, SparseCore 0:
  13.0 213.0 all-reduce.6
  255.5 36.9 reduce-scatter.2
  294.7 19.6 all-gather.2
  323.8 37.9 reduce-scatter.4
  364.3 19.6 all-gather.4
  388.1 75.5 all-reduce.4
where the time goes:
time: 486 us; the launch traced here: 484 us
  waiting for transfers between devices  329 us (68%)
  local copies, waits for them, and re-layouts  48.9 us (10%)
  matrix products  45 us (9%)
  other arithmetic  40.1 us (8%)
  between operations  14.3 us (3%)
  blocking collectives  7.15 us (1%)
    psum x1, waiting for transfers between devices, spread_2(): return lax.psum(kept, axis)  191 us
    psum x1, waiting for transfers between devices, row_sums(): return lax.psum(pieces_in, 'row')  77.7 us
    reduce_scatter x2, waiting for transfers between devices, finish(): lax.psum_scatter(partial_value, 'col', scatter_dimension=0, tiled=True)  44.8 us
    dot_general x2, matrix products, partial_product(): jnp.dot(row_slab, spread.reshape(col_blocks * BS, W), preferred_element_t...  21.2 us
    gather x2, local copies, waits for them, and re-layouts, partial_product(): jnp.take(slab_blocks, own_rows, axis=0)  19.1 us
    select_n x3, other arithmetic, partial_product(): jnp.take(slab_blocks, own_rows, axis=0)  16.8 us
    all_gather x2, waiting for transfers between devices, finish(): return lax.all_gather(share_out, 'col', axis=0, tiled=True)  14.9 us
    another operation x3, other arithmetic, partial_product(): received = jnp.stack(pieces).reshape(fanout * PAD, BS * W)  11.9 us
  transfers between devices with their start and end apart: 6, of which 5 were waited for; matrix products, arithmetic and copies ran while one was open for 18% of the time, Pallas kernels for 0%

commit v1 on v0

--- a/solution.py
+++ b/solution.py
@@ -9,9 +9,15 @@
 PAD = 12
 
 
+def summed_here(value, axis):
+    parts = lax.all_gather(value, axis, axis=0, tiled=False)
+    result = parts.sum(axis=0)
+    return result
+
+
 def spread_2(value, axis, source):
     kept = jnp.where(lax.axis_index(axis) == source, value, 0).astype(value.dtype)
-    return lax.psum(kept, axis)
+    return summed_here(kept, axis)
 
 
 def contract_rows(former, latter):

time: 486 us -> 952 us (1.96)
  waiting for transfers between devices: 329 us -> 759 us
  other arithmetic: 40.1 us -> 73.1 us
    all_gather x0 -> x4, waiting for transfers between devices: none -> 609 us  [summed_here(): parts = lax.all_gather(value, axis, axis=0, tiled=False)]
    psum x1 -> x0, waiting for transfers between devices: 191 us -> none  [spread_2(): return lax.psum(kept, axis)]
    reduce_sum x0 -> x4, other arithmetic: none -> 31.9 us  [summed_here(): result = parts.sum(axis=0)]
    reduce_scatter x2, waiting for transfers between devices: 44.8 us -> 56 us  [finish(): lax.psum_scatter(partial_value, 'col', scatter_dimension=0, tiled=True)]
  transfers between devices with their start and end apart: 6 -> 9, of which waited for: 5 -> 8; matrix products, arithmetic and copies ran while one was open for 18% -> 16% of each run, Pallas kernels for 0% -> 0%
where the time goes in v1:
time: 952 us; the launch traced here: 950 us
  waiting for transfers between devices  759 us (80%)
  other arithmetic  73.1 us (8%)
  local copies, waits for them, and re-layouts  49.5 us (5%)
  matrix products  47 us (5%)
  between operations  14 us (1%)
    all_gather x4, waiting for transfers between devices, summed_here(): parts = lax.all_gather(value, axis, axis=0, tiled=False)  609 us
    psum x1, waiting for transfers between devices, row_sums(): return lax.psum(pieces_in, 'row')  77.8 us
    reduce_scatter x2, waiting for transfers between devices, finish(): lax.psum_scatter(partial_value, 'col', scatter_dimension=0, tiled=True)  56 us
    reduce_sum x4, other arithmetic, summed_here(): result = parts.sum(axis=0)  31.9 us
    dot_general x2, matrix products, partial_product(): jnp.dot(row_slab, spread.reshape(col_blocks * BS, W), preferred_element_t...  21.4 us
    gather x2, local copies, waits for them, and re-layouts, partial_product(): jnp.take(slab_blocks, own_rows, axis=0)  19.1 us
  transfers between devices with their start and end apart: 9, of which 8 were waited for; matrix products, arithmetic and copies ran while one was open for 16% of the time, Pallas kernels for 0%

profile of v1, /device:TPU:0, one launch (start us, length us, event | category | flops | bytes accessed | tf_op | source)
XLA Modules:
  0.0 950.2 jit_solution(14562580066250098571)
XLA Ops:
  15.4 9.8 %gather_fusion = bf16[12,128,3072]{2,1,0:T(8,128)(2,1)} fusion(bf16[12,128,3072]{2,1,0:T(8,128)(2,1)} %bitcast.59, s32[1024]{0:T(1024)S(1)} %pad_clamp_fusion.1), kind=kCustom, calls=%fused_computation.clone | custom fusion | bytes 18874416 | tf_op jit(solution)/shard_map/jit(_take)/gather | solution.py:55
  28.8 8.3 broadcast_select_fusion.1
  37.0 152.6 %all-gather.17.cloned.1.call-done = bf16[12288,512]{1,0:T(8,128)(2,1)} async-done(((bf16[1536,512]{1,0:T(8,128)(2,1)}), bf16[12288,512]{1,0:T(8,128)(2,1)}) %all-gather.17.cloned.1.call-update) | async-done | bytes 12582928 | tf_op jit(solution)/shard_map/all_gather | solution.py:13
  189.7 8.0 reduce_sum.49
  197.6 169.1 %all-gather.15.cloned.1.call-done = bf16[12288,512]{1,0:T(8,128)(2,1)} async-done(((bf16[1536,512]{1,0:T(8,128)(2,1)}), bf16[12288,512]{1,0:T(8,128)(2,1)}) %all-gather.15.cloned.1.call-update) | async-done | bytes 12582928 | tf_op jit(solution)/shard_map/all_gather | solution.py:13
  366.7 8.0 reduce_sum.48
  379.1 5.1 reshape.70
  384.3 4.6 convolution_convert_fusion.1
  388.9 5.2 reshape.71
  394.0 10.8 %fusion.53 = f32[1536,512]{1,0:T(8,128)} fusion(bf16[1536,3072]{1,0:T(8,128)(2,1)} %bitcast.66, bf16[3072,512]{1,0:T(8,128)(2,1)} %reshape.71), kind=kOutput, calls=%fused_computation.96 | convolution fusion | flops 4831838208 | bytes 15728640 | tf_op jit(solution)/shard_map/dot_general | solution.py:75
  405.7 9.3 gather_fusion.1
  416.4 8.2 broadcast_select_fusion
  424.7 118.6 %all-gather.19.cloned.1.call-done = bf16[12288,512]{1,0:T(8,128)(2,1)} async-done(((bf16[1536,512]{1,0:T(8,128)(2,1)}), bf16[12288,512]{1,0:T(8,128)(2,1)}) %all-gather.19.cloned.1.call-update) | async-done | bytes 12582928 | tf_op jit(solution)/shard_map/all_gather | solution.py:13
  543.3 8.0 reduce_sum.50
  551.2 168.4 %all-gather.21.cloned.1.call-done = bf16[12288,512]{1,0:T(8,128)(2,1)} async-done(((bf16[1536,512]{1,0:T(8,128)(2,1)}), bf16[12288,512]{1,0:T(8,128)(2,1)}) %all-gather.21.cloned.1.call-update) | async-done | bytes 12582928 | tf_op jit(solution)/shard_map/all_gather | solution.py:13
  719.6 8.0 reduce_sum.51
  727.6 30.5 %reduce-scatter.3.cloned.1.call-done = f32[384,512]{1,0:T(8,128)} async-done(((f32[1536,512]{1,0:T(8,128)}), f32[384,512]{1,0:T(8,128)}) %reduce-scatter.3.cloned.1.call-update) | async-done | bytes 786448 | tf_op jit(solution)/shard_map/reduce_scatter | solution.py:81
  764.1 5.2 reshape.73
  773.8 5.2 reshape.74
  779.0 10.7 %fusion.54 = f32[1536,512]{1,0:T(8,128)} fusion(bf16[1536,3072]{1,0:T(8,128)(2,1)} %bitcast.65, bf16[3072,512]{1,0:T(8,128)(2,1)} %reshape.74), kind=kOutput, calls=%fused_computation.97 | convolution fusion | flops 4831838208 | bytes 15728640 | tf_op jit(solution)/shard_map/dot_general | solution.py:75
  802.2 25.5 %reduce-scatter.5.cloned.1.call-done = f32[384,512]{1,0:T(8,128)} async-done(((f32[1536,512]{1,0:T(8,128)}), f32[384,512]{1,0:T(8,128)}) %reduce-scatter.5.cloned.1.call-update) | async-done | bytes 786448 | tf_op jit(solution)/shard_map/reduce_scatter | solution.py:81
  835.0 14.9 %all-gather.13.cloned.1.call-done = bf16[1536,512]{1,0:T(8,128)(2,1)} async-done(((bf16[384,512]{1,0:T(8,128)(2,1)}), bf16[1536,512]{1,0:T(8,128)(2,1)}) %all-gather.13.cloned.1.call-update) | async-done | bytes 1572880 | tf_op jit(solution)/shard_map/all_gather | solution.py:86
  852.0 77.8 %all-reduce.3.cloned.1.call-done = (f32[128,512]{1,0:T(8,128)}, f32[128,512]{1,0:T(8,128)}, f32[128,512]{1,0:T(8,128)}) async-done(((f32[128,512]{1,0:T(8,128)}, f32[128,512]{1,0:T(8,128)}, f32[128,512]{1,0:T(8,128)}), (f32[128,512]{1,0:T(8,128)}, f32[128,512]{1,0:T(8,128)}, f32[128,512]{1,0:T(8,128)})) %all-reduce.3.cloned.1.call-update) | async-done | bytes 786448 | tf_op jit(solution)/shard_map/psum | solution.py:89
  932.3 7.2 all_gather.43
  (82 shorter events, 57.4 us)
Async XLA Ops:
  7.2 820.5 %copy-start = (bf16[512,512]{1,0:T(8,128)(2,1)S(1)}, bf16[512,512]{1,0:T(8,128)(2,1)}, u32[]{:S(2)}) copy-start(bf16[512,512]{1,0:T(8,128)(2,1)} %param.19) | copy-start | bytes 1572868
  7.2 182.5 %all-gather.17.cloned.1.call-start = ((), (), s32[]{:S(2)}) async-start(), calls=%async_computation.7 | async-start | bytes 14155776 | tf_op jit(solution)/shard_map/all_gather | solution.py:13
  7.2 4.2 copy-start.1
  10.7 356.1 %all-gather.15.cloned.1.call-start = ((), (), s32[]{:S(2)}) async-start(), calls=%async_computation.6 | async-start | bytes 14155776 | tf_op jit(solution)/shard_map/all_gather | solution.py:13
  11.4 531.8 %all-gather.19.cloned.1.call-start = ((), (), s32[]{:S(2)}) async-start(), calls=%async_computation.8 | async-start | bytes 14155776 | tf_op jit(solution)/shard_map/all_gather | solution.py:13
  13.4 706.3 %all-gather.21.cloned.1.call-start = ((), (), s32[]{:S(2)}) async-start(), calls=%async_computation.9 | async-start | bytes 14155776 | tf_op jit(solution)/shard_map/all_gather | solution.py:13
  13.9 744.2 %reduce-scatter.3.cloned.1.call-start = ((), (), s32[]{:S(2)}) async-start(), calls=%async_computation.2 | async-start | bytes 3932160 | tf_op jit(solution)/shard_map/reduce_scatter | solution.py:81
  15.4 9.8 %copy-start.8 = (s32[8]{0:T(128)S(1)}, s32[8]{0:T(128)}, u32[]{:S(2)}) copy-start(s32[8]{0:T(128)} %param.17) | copy-start | bytes 100
  15.4 9.8 %copy-start.9 = (s32[8]{0:T(128)S(1)}, s32[8]{0:T(128)}, u32[]{:S(2)}) copy-start(s32[8]{0:T(128)} %param.14) | copy-start | bytes 100
  404.8 387.1 %all-gather.11.cloned.1.call-start = ((), (), s32[]{:S(2)}) async-start(), calls=%async_computation.3 | async-start | bytes 1966080 | tf_op jit(solution)/shard_map/all_gather | solution.py:86
  760.2 67.6 %reduce-scatter.5.cloned.1.call-start = ((), (), s32[]{:S(2)}) async-start(), calls=%async_computation.4 | async-start | bytes 3932160 | tf_op jit(solution)/shard_map/reduce_scatter | solution.py:81
  789.7 60.2 %all-gather.13.cloned.1.call-start = ((), (), s32[]{:S(2)}) async-start(), calls=%async_computation.5 | async-start | bytes 1966080 | tf_op jit(solution)/shard_map/all_gather | solution.py:86
  830.1 99.7 %all-reduce.3.cloned.1.call-start = ((), (), s32[]{:S(2)}) async-start(), calls=%async_computation.10 | async-start | bytes 1572864 | tf_op jit(solution)/shard_map/psum | solution.py:89
  832.3 97.6 %copy-start.6 = (f32[128,512]{1,0:T(8,128)S(1)}, f32[128,512]{1,0:T(8,128)}, u32[]{:S(2)}) copy-start(f32[128,512]{1,0:T(8,128)} %param.20) | copy-start | bytes 786436
  835.0 104.5 %copy-start.7 = (f32[128,512]{1,0:T(8,128)S(1)}, f32[128,512]{1,0:T(8,128)}, u32[]{:S(2)}) copy-start(f32[128,512]{1,0:T(8,128)} %param.21) | copy-start | bytes 786436
  852.0 89.4 %copy-start.2 = (bf16[1536,512]{1,0:T(8,128)(2,1)S(1)}, bf16[1536,512]{1,0:T(8,128)(2,1)}, u32[]{:S(2)}) copy-start(bf16[1536,512]{1,0:T(8,128)(2,1)} %all-gather.11.cloned.1.call-done) | copy-start | bytes 4718596
  930.8 11.7 %copy-start.4 = (f32[128,512]{1,0:T(8,128)}, f32[128,512]{1,0:T(8,128)S(1)}, u32[]{:S(2)}) copy-start(f32[128,512]{1,0:T(8,128)S(1)} %sub.9) | copy-start | bytes 786436
  930.9 11.7 %copy-start.3 = (bf16[1536,512]{1,0:T(8,128)(2,1)S(1)}, bf16[1536,512]{1,0:T(8,128)(2,1)}, u32[]{:S(2)}) copy-start(bf16[1536,512]{1,0:T(8,128)(2,1)} %all-gather.13.cloned.1.call-done) | copy-start | bytes 4718596
  932.3 11.4 %copy-start.5 = (bf16[128,512]{1,0:T(8,128)(2,1)}, bf16[128,512]{1,0:T(8,128)(2,1)S(1)}, u32[]{:S(2)}) copy-start(bf16[128,512]{1,0:T(8,128)(2,1)S(1)} %fusion.4) | copy-start | bytes 393220
Sparse Core Ops, SparseCore 0:
  10.8 178.8 all-gather.16
  192.4 174.2 all-gather.14
  368.9 174.2 all-gather.18
  545.3 174.2 all-gather.20
  722.0 36.0 reduce-scatter.2
  760.3 19.6 all-gather.10
  789.8 37.8 reduce-scatter.4
  830.2 19.6 all-gather.12
  854.2 75.5 all-reduce.2
